TPU v7x, 32 devices: a whole 2x2x4 slice. The times are simulated.
32 devices in a mesh: front: 1, row: 16 (over z, y, x), col: 2 (over core).
Axes of the slice: x: 2, y: 2, z: 4, core: 2. Of those that a mesh axis runs over, the one named last changes fastest.
Arguments:
- contributions: float32 [16, 128, 4096], P(('front', 'row'), None, 'col'), may hold values from -0.176776695 to 0.176776695
- valid_rows: int32 [16], P(('front', 'row')), may hold values from 1 to 128, 1280 in all
Outputs:
- r_rows: float32 [512, 4096], P('front', 'col')
All inputs are finite; a program needn't handle non-finite values. No bound on the sum of `valid_rows` on one device may be relied on, other than what follows from the above.
Results may differ from a plain program's by a relative error of at most 0.0003.
Values sent between devices are 32-bit elements; how exact they have to be, the bound alone decides.
A program may use at most 64 MiB of HBM per device.

v0:
```python
import jax
import jax.numpy as jnp
from jax import lax
from jax.sharding import PartitionSpec as P

PANEL = 256
NPANEL = 2


def spread(block, axis, owner):
    block = jnp.where(lax.axis_index(axis) == owner, block, jnp.zeros_like(block))
    return lax.psum(block, axis)


def inner_cols(left, right):
    return jnp.einsum("rp,rc->pc", left, right, precision=lax.Precision.HIGHEST)


def lower_factor(gram):
    return jnp.linalg.cholesky(gram)


def lower_inverse(factor):
    identity = jnp.eye(factor.shape[0], dtype=jnp.float32)
    return jax.scipy.linalg.solve_triangular(factor, identity, lower=True)


def body(contributions, valid_rows):
    blocks, height, width_local = contributions.shape
    live_rows = (jnp.arange(height, dtype=jnp.int32)[None, :] < valid_rows[:, None]).astype(
        jnp.float32
    )
    frontal = (contributions * live_rows[:, :, None]).reshape(blocks * height, width_local)
    leading = NPANEL * PANEL
    leading_cols = spread(frontal[:, :leading], "col", 0)
    gram_total = lax.psum(inner_cols(leading_cols, leading_cols), "row")
    inverse = lower_inverse(lower_factor(gram_total))
    first_basis = jnp.dot(leading_cols, inverse.T, precision=lax.Precision.HIGHEST)
    projected = lax.psum(inner_cols(first_basis, frontal), "row")
    column_ids = lax.axis_index("col") * width_local + jnp.arange(width_local, dtype=jnp.int32)
    kept_mask = column_ids[None, :] >= jnp.arange(leading, dtype=jnp.int32)[:, None]
    return jnp.where(kept_mask, projected, jnp.zeros_like(projected))


def solution(mesh):
    return jax.shard_map(
        body,
        mesh=mesh,
        in_specs=(P(("front", "row"), None, "col"), P(("front", "row"))),
        out_specs=P("front", "col"),
        check_vma=False,
    )
```

profile of v0, /device:TPU:0, one launch (start us, length us, event | category | flops | bytes accessed | tf_op | source)
XLA Modules:
  0.0 487.8 jit_solution(4547117279546331932)
XLA Ops:
  7.2 1.4 multiply_bitcast_fusion
  9.4 21.3 %all-reduce.5.cloned.1.call-done = f32[128,512]{1,0:T(8,128)} async-done(((f32[128,512]{1,0:T(8,128)}), f32[128,512]{1,0:T(8,128)}) %all-reduce.5.cloned.1.call-update) | async-done | bytes 262160 | tf_op jit(solution)/shard_map/psum | solution.py:12
  30.6 3.0 fusion.42
  34.7 114.8 %all-reduce.7.cloned.1.call-done = f32[512,512]{0,1:T(8,128)} async-done(((f32[512,512]{0,1:T(8,128)}), f32[512,512]{0,1:T(8,128)}) %all-reduce.7.cloned.1.call-update) | async-done | bytes 1048592 | tf_op jit(solution)/shard_map/psum | solution.py:36
  149.5 1.6 copy.4
  151.1 1.4 fusion.9
  153.5 11.7 %cholesky.104 = f32[128,128]{1,0:T(8,128)S(1)} custom-call(f32[128,128]{1,0:T(8,128)S(1)} %cholesky.266), custom_call_target="Cholesky" | custom-call | tf_op jit(solution)/shard_map/jit(cholesky)/cholesky | solution.py:20
  165.3 9.8 %custom-call.31 = f32[1,128,128]{1,2,0:T(8,128)S(1)} custom-call(f32[1,128,128]{2,1,0:T(8,128)S(1)} %get-tuple-element.32), custom_call_target="InvertDiagBlocksLowerTriangular" | custom-call | tf_op jit(solution)/shard_map/jit(cholesky)/cholesky | solution.py:20
  175.2 1.2 constant_dynamic-update-slice_fusion.3
  176.4 1.3 convolution_subtract_fusion.3
  177.7 11.7 %cholesky.217 = f32[128,128]{1,0:T(8,128)S(1)} custom-call(f32[128,128]{1,0:T(8,128)S(1)} %cholesky.270), custom_call_target="Cholesky" | custom-call | tf_op jit(solution)/shard_map/jit(cholesky)/cholesky | solution.py:20
  189.5 9.9 %custom-call.32 = f32[1,128,128]{1,2,0:T(8,128)S(1)} custom-call(f32[1,128,128]{2,1,0:T(8,128)S(1)} %get-tuple-element.29), custom_call_target="InvertDiagBlocksLowerTriangular" | custom-call | tf_op jit(solution)/shard_map/jit(cholesky)/cholesky | solution.py:20
  199.7 1.3 convolution_subtract_fusion.4
  201.0 11.7 %cholesky.238 = f32[128,128]{1,0:T(8,128)S(1)} custom-call(f32[128,128]{1,0:T(8,128)S(1)} %cholesky.275), custom_call_target="Cholesky" | custom-call | tf_op jit(solution)/shard_map/jit(cholesky)/cholesky | solution.py:20
  213.4 9.8 %custom-call.33 = f32[1,128,128]{1,2,0:T(8,128)S(1)} custom-call(f32[1,128,128]{2,1,0:T(8,128)S(1)} %get-tuple-element.26), custom_call_target="InvertDiagBlocksLowerTriangular" | custom-call | tf_op jit(solution)/shard_map/jit(cholesky)/cholesky | solution.py:20
  223.5 1.2 convolution_subtract_fusion.5
  224.7 11.7 %cholesky.255 = f32[128,128]{1,0:T(8,128)S(1)} custom-call(f32[128,128]{1,0:T(8,128)S(1)} %convolution_subtract_fusion.5), custom_call_target="Cholesky" | custom-call | tf_op jit(solution)/shard_map/jit(cholesky)/cholesky | solution.py:20
  240.5 1.1 select_select_fusion
  241.6 14.1 %while.1 = (s32[]{:T(128)}, f32[512,512]{1,0:T(8,128)}, s32[4,2]{0,1:T(2,128)S(1)}, f32[4,128,128]{2,1,0:T(8,128)}, s32[]{:T(128)}) while((s32[]{:T(128)}, f32[512,512]{1,0:T(8,128)}, s32[4,2]{0,1:T(2,128)S(1)}, f32[4,128,128]{2,1,0:T(8,128)}, s32[]{:T(128)}) %tuple.27), condition=%wide.while_cond, body=%wide.while_body.sunk | while | flops 2 | bytes 132705 | solution.py:25
  242.3 2.9 bitcast_dynamic-update-slice_fusion.2
  245.8 2.9 bitcast_dynamic-update-slice_fusion.2
  249.4 2.9 bitcast_dynamic-update-slice_fusion.2
  252.9 2.8 bitcast_dynamic-update-slice_fusion.2
  255.7 40.1 %custom-call.34 = f32[4,128,128]{1,2,0:T(8,128)S(1)} custom-call(f32[4,128,128]{2,1,0:T(8,128)} %get-tuple-element.12), custom_call_target="InvertDiagBlocksLowerTriangular" | custom-call | tf_op jit(solution)/shard_map/jit(_solve_triangular)/triangular_solve | solution.py:25
  295.8 1.1 fusion.20
  296.9 1.2 convolution_subtract_fusion.1
  298.6 1.3 convolution_subtract_fusion
  300.3 1.6 convolution_subtract_fusion.2
  302.4 1.2 fusion.1
  303.5 5.0 %fusion.43 = f32[512,2048]{1,0:T(8,128)} fusion(f32[128,512]{1,0:T(8,128)S(1)} %fusion.1, f32[128,2048]{1,0:T(8,128)S(1)} %multiply_bitcast_fusion), kind=kOutput, calls=%fused_computation.84 | convolution fusion | flops 1610612736 | bytes 5505024 | tf_op jit(solution)/shard_map/rp,rc->pc/dot_general | solution.py:16
  308.6 167.5 %all-reduce.9.cloned.1.call-done = f32[512,2048]{1,0:T(8,128)} async-done(((f32[512,2048]{1,0:T(8,128)}), f32[512,2048]{1,0:T(8,128)}) %all-reduce.9.cloned.1.call-update) | async-done | bytes 4194320 | tf_op jit(solution)/shard_map/psum | solution.py:39
  476.1 5.1 %fusion = f32[512,2048]{1,0:T(8,128)} fusion(f32[512,2048]{1,0:T(8,128)} %all-reduce.9.cloned.1.call-done, s32[2048]{0:T(1024)S(1)} %iota_add_fusion), kind=kLoop, calls=%fused_computation.3 | loop fusion | flops 2097152 | bytes 8396800 | tf_op jit(solution)/shard_map/jit(_where)/select_n | solution.py:42
  (42 shorter events, 9.7 us)
Async XLA Ops:
  6.5 24.1 %all-reduce.5.cloned.1.call-start = ((), (), s32[]{:S(2)}) async-start(), calls=%async_computation | async-start | bytes 524288 | tf_op jit(solution)/shard_map/psum | solution.py:12
  9.3 140.2 %all-reduce.7.cloned.1.call-start = ((), (), s32[]{:S(2)}) async-start(), calls=%async_computation.1 | async-start | bytes 2097152 | tf_op jit(solution)/shard_map/psum | solution.py:36
  33.7 442.4 %all-reduce.9.cloned.1.call-start = ((), (), s32[]{:S(2)}) async-start(), calls=%async_computation.2 | async-start | bytes 8388608 | tf_op jit(solution)/shard_map/psum | solution.py:39
  152.5 1.0 copy-start
  240.5 61.9 %copy-start.1 = (f32[128,512]{1,0:T(8,128)S(1)}, f32[128,512]{1,0:T(8,128)}, u32[]{:S(2)}) copy-start(f32[128,512]{1,0:T(8,128)} %all-reduce.5.cloned.1.call-done) | copy-start | bytes 786436
Sparse Core Ops, SparseCore 0:
  9.7 20.9 all-reduce.4
  35.9 113.5 all-reduce.6
  308.7 167.3 all-reduce.8
where the time goes:
time: 489 us; the launch traced here: 488 us
  waiting for transfers between devices  304 us (62%)
  other arithmetic  130 us (27%)
  matrix products  21.1 us (4%)
  local copies, waits for them, and re-layouts  16.8 us (3%)
  between operations  16.6 us (3%)
    psum x1, waiting for transfers between devices, body(): projected = lax.psum(inner_cols(first_basis, frontal), 'row')  168 us
    psum x1, waiting for transfers between devices, body(): gram_total = lax.psum(inner_cols(leading_cols, leading_cols), 'row')  115 us
    another operation x14, other arithmetic, lower_factor(): return jnp.linalg.cholesky(gram)  78.8 us
    another operation x3, other arithmetic, lower_inverse(): return jax.scipy.linalg.solve_triangular(factor, identity, lower=True)  41.2 us
    psum x1, waiting for transfers between devices, spread(): return lax.psum(block, axis)  21.3 us
    another operation x12, local copies, waits for them, and re-layouts  14.1 us
  transfers between devices with their start and end apart: 3, of which 3 were waited for; matrix products, arithmetic and copies ran while one was open for 0% of the time, Pallas kernels for 0%

commit v1 on v0

v1 whole, which is shorter than its diff:
```python
import functools

import jax
import jax.numpy as jnp
from jax import lax
from jax.experimental import pallas as pl
from jax.experimental.pallas import tpu as pltpu
from jax.sharding import PartitionSpec as P

PANEL = 256
NPANEL = 2
LANES = 128
SUB = 8
HIGHEST = lax.Precision.HIGHEST
MESH = pl.DeviceIdType.MESH


def spread(block, axis, owner):
    block = jnp.where(lax.axis_index(axis) == owner, block, jnp.zeros_like(block))
    return lax.psum(block, axis)


def inner_cols(left, right):
    return jnp.einsum("rp,rc->pc", left, right, precision=HIGHEST)


def by_psum(frontal, leading):
    width_local = frontal.shape[1]
    leading_cols = spread(frontal[:, :leading], "col", 0)
    gram_total = lax.psum(inner_cols(leading_cols, leading_cols), "row")
    factor = jnp.linalg.cholesky(gram_total)
    identity = jnp.eye(leading, dtype=jnp.float32)
    inverse = jax.scipy.linalg.solve_triangular(factor, identity, lower=True)
    first_basis = jnp.dot(leading_cols, inverse.T, precision=HIGHEST)
    projected = lax.psum(inner_cols(first_basis, frontal), "row")
    column_ids = lax.axis_index("col") * width_local + jnp.arange(width_local, dtype=jnp.int32)
    kept_mask = column_ids[None, :] >= jnp.arange(leading, dtype=jnp.int32)[:, None]
    return jnp.where(kept_mask, projected, jnp.zeros_like(projected))


def dot_t(left, right):
    return lax.dot_general(
        left, right, (((0,), (0,)), ((), ())), precision=HIGHEST, preferred_element_type=jnp.float32
    )


def inverse_factor(read, hooks):
    groups = LANES // SUB
    row = lax.broadcasted_iota(jnp.int32, (SUB, LANES), 0)
    col = lax.broadcasted_iota(jnp.int32, (SUB, LANES), 1)
    a = [read(g) for g in range(groups)]
    b = [jnp.where(row + g * SUB == col, 1.0, 0.0).astype(jnp.float32) for g in range(groups)]
    scales = []
    for j in range(LANES):
        if j in hooks:
            hooks[j]()
        home, i = divmod(j, SUB)
        prow = a[home][i : i + 1, :]
        brow = b[home][i : i + 1, :]
        pinv = 1.0 / prow[:, j : j + 1]
        srow = prow * pinv
        trow = brow * pinv
        for g in range(home, groups):
            f = a[g][:, j : j + 1]
            if g == home:
                if i == SUB - 1:
                    continue
                f = jnp.where(row > i, jnp.broadcast_to(f, (SUB, LANES)), 0.0)
            a[g] = a[g] - f * srow
            b[g] = b[g] - f * trow
        if i == SUB - 1:
            diag = jnp.sum(jnp.where(row + home * SUB == col, a[home], 0.0), axis=1, keepdims=True)
            b[home] = b[home] * lax.rsqrt(diag)
    return b


def kernel(n, leading, f_ref, out_ref, a_all, f_all, gc, inv,
           own_sem, pair_send, pair_recv, ag_send, ag_recv, core_send, core_recv,
           x_send, x_recv, r_send, r_recv):
    height, width = f_ref.shape
    share = width // n
    half = height // 2
    chunks = leading // LANES
    stages = n.bit_length() - 1
    r = lax.axis_index("row")
    c = lax.axis_index("col")
    bits = [n >> (s + 1) for s in range(stages)]
    deltas = [b * (1 - 2 * (lax.rem(r // b, 2))) for b in bits]

    def ordered(parity):
        return deltas[:-2] + [
            deltas[-2] * (1 - parity) + deltas[-1] * parity,
            deltas[-1] * (1 - parity) + deltas[-2] * parity,
        ]

    def at(j, steps):
        place = r
        for s in range(stages):
            if (j >> s) & 1:
                place = place + steps[s]
        return place

    barrier = pltpu.get_barrier_semaphore()
    for d in range(1, n):
        pl.semaphore_signal(barrier, inc=1, device_id={"row": lax.rem(r + d, n)}, device_id_type=MESH)
    pl.semaphore_signal(barrier, inc=1, device_id={"col": 1 - c}, device_id_type=MESH)
    pl.semaphore_wait(barrier, n)

    mine = pl.ds(pl.multiple_of(r * height, height), height)
    lead = f_ref.at[:, pl.ds(0, leading)]
    own_lead = pltpu.make_async_copy(lead, a_all.at[mine, :], own_sem.at[0])
    to_pair = pltpu.make_async_remote_copy(
        src_ref=lead, dst_ref=a_all.at[mine, :], send_sem=pair_send, recv_sem=pair_recv,
        device_id={"col": 1 - c}, device_id_type=MESH,
    )

    @pl.when(c == 0)
    def _():
        to_pair.start()
        own_lead.start()
        own_lead.wait()

    @pl.when(c == 1)
    def _():
        to_pair.wait_recv()

    lead_steps = ordered(c)

    def lead_half(j, core):
        start = at(j, lead_steps) * height + core * half
        return a_all.at[pl.ds(pl.multiple_of(start, half), half), :]

    def lead_copy(j, s):
        return pltpu.make_async_remote_copy(
            src_ref=lead_half(j, c), dst_ref=lead_half(j, c),
            send_sem=ag_send.at[j + (1 << s)], recv_sem=ag_recv.at[j + (1 << s)],
            device_id={"row": r + lead_steps[s]}, device_id_type=MESH,
        )

    def core_copy(j):
        return pltpu.make_async_remote_copy(
            src_ref=lead_half(j, c), dst_ref=lead_half(j, c),
            send_sem=core_send.at[j], recv_sem=core_recv.at[j],
            device_id={"col": 1 - c}, device_id_type=MESH,
        )

    def share_copy(d):
        peer = lax.rem(r + d, n)
        return pltpu.make_async_remote_copy(
            src_ref=f_ref.at[:, pl.ds(pl.multiple_of(peer * share, share), share)],
            dst_ref=f_all.at[mine, :],
            send_sem=x_send.at[d], recv_sem=x_recv.at[d],
            device_id={"row": peer}, device_id_type=MESH,
        )

    for s in range(stages):
        lead_copy(0, s).start()
    own_share = pltpu.make_async_copy(
        f_ref.at[:, pl.ds(pl.multiple_of(r * share, share), share)], f_all.at[mine, :], own_sem.at[1]
    )
    own_share.start()
    for d in range(1, n):
        share_copy(d).start()
    for j in range(1, n):
        top = j.bit_length() - 1
        lead_copy(j - (1 << top), top).wait_recv()
        for s in range(top + 1, stages):
            lead_copy(j, s).start()
        core_copy(j).start()
    own_share.wait()
    for j in range(1, n):
        core_copy(j).wait_recv()
    for d in range(1, n):
        share_copy(d).wait_recv()

    step_rows = 4 * LANES
    gc[...] = jnp.zeros_like(gc)

    @pl.loop(0, (n * height) // step_rows)
    def _(t):
        rows = pl.ds(pl.multiple_of(t * step_rows, step_rows), step_rows)
        right = f_all[rows, :]
        for k in range(chunks):
            ks = pl.ds(k * LANES, LANES)
            left = a_all[rows, ks]
            rest = pl.ds(k * LANES, leading - k * LANES)
            gc[ks, rest] += dot_t(left, a_all[rows, rest])
            gc[ks, pl.ds(leading, share)] += dot_t(left, right)

    def out_piece(k, j, steps):
        cols = pl.ds(pl.multiple_of(at(j, steps) * share, share), share)
        return out_ref.at[pl.ds(pl.multiple_of(k * LANES, LANES), LANES), cols]

    def out_copy(k, j, s):
        steps = ordered(lax.rem(k, 2))
        return pltpu.make_async_remote_copy(
            src_ref=out_piece(k, j, steps), dst_ref=out_piece(k, j, steps),
            send_sem=r_send.at[k, j + (1 << s)], recv_sem=r_recv.at[k, j + (1 << s)],
            device_id={"row": r + steps[s]}, device_id_type=MESH,
        )

    def forward(k, top):
        for j in range(1 << top, 2 << top):
            out_copy(k, j - (1 << top), top).wait_recv()
            for s in range(top + 1, stages):
                out_copy(k, j, s).start()

    first_col = c * width + r * share
    row_id = lax.broadcasted_iota(jnp.int32, (LANES, share), 0)
    col_id = lax.broadcasted_iota(jnp.int32, (LANES, share), 1) + first_col

    @pl.loop(0, chunks)
    def _(k):
        base = pl.multiple_of(k * LANES, LANES)
        ks = pl.ds(base, LANES)

        def read(g):
            return gc[pl.ds(pl.multiple_of(base + g * SUB, SUB), SUB), ks]

        def hook(top):
            def run():
                @pl.when(k > 0)
                def _():
                    forward(k - 1, top)
            return run

        gap = LANES // stages
        hooks = {gap * (s + 1) - 1: hook(s) for s in range(stages)}
        b = inverse_factor(read, hooks)
        for g, part in enumerate(b):
            inv[pl.ds(g * SUB, SUB), :] = part
        rows = jnp.dot(inv[...], gc[ks, :], precision=HIGHEST, preferred_element_type=jnp.float32)
        mine_out = rows[:, leading:]
        out_ref[ks, pl.ds(pl.multiple_of(r * share, share), share)] = jnp.where(
            col_id >= row_id + base, mine_out, 0.0
        )
        for s in range(stages):
            out_copy(k, 0, s).start()
        gc[ks, :] = rows
        for i in range(1, chunks):
            @pl.when(i > k)
            def _():
                left = gc[ks, pl.ds(i * LANES, LANES)]
                rest = pl.ds(i * LANES, leading + share - i * LANES)
                gc[pl.ds(i * LANES, LANES), rest] -= dot_t(left, gc[ks, rest])

    for top in range(stages):
        forward(chunks - 1, top)

    @pl.when(c == 0)
    def _():
        to_pair.wait_send()

    for j in range(1, n):
        top = j.bit_length() - 1
        lead_copy(j - (1 << top), top).wait_send()
        core_copy(j).wait_send()
        share_copy(j).wait_send()
        for k in range(chunks):
            out_copy(k, j - (1 << top), top).wait_send()


def by_kernel(frontal, leading, n):
    height, width = frontal.shape
    share = width // n
    dma = pltpu.SemaphoreType.DMA
    return pl.pallas_call(
        functools.partial(kernel, n, leading),
        out_shape=jax.ShapeDtypeStruct((leading, width), jnp.float32),
        in_specs=[pl.BlockSpec(memory_space=pltpu.VMEM)],
        out_specs=pl.BlockSpec(memory_space=pltpu.VMEM),
        scratch_shapes=[
            pltpu.VMEM((n * height, leading), jnp.float32),
            pltpu.VMEM((n * height, share), jnp.float32),
            pltpu.VMEM((leading, leading + share), jnp.float32),
            pltpu.VMEM((LANES, LANES), jnp.float32),
            dma((2,)), dma, dma, dma((n,)), dma((n,)), dma((n,)), dma((n,)),
            dma((n,)), dma((n,)),
            dma((leading // LANES, n)), dma((leading // LANES, n)),
        ],
        compiler_params=pltpu.CompilerParams(
            collective_id=0, has_side_effects=True, vmem_limit_bytes=48 << 20
        ),
        name="front_rows",
    )(frontal)


def body(n, pair, contributions, valid_rows):
    blocks, height, width_local = contributions.shape
    live_rows = jnp.arange(height, dtype=jnp.int32)[None, :] < valid_rows[:, None]
    frontal = jnp.where(live_rows[:, :, None], contributions, 0.0).reshape(blocks * height, width_local)
    leading = NPANEL * PANEL
    rows = blocks * height
    fits = (
        pair == 2 and n >= 4 and n & (n - 1) == 0 and width_local % n == 0
        and width_local // n == LANES and rows == LANES and leading <= width_local
    )
    if fits:
        return by_kernel(frontal, leading, n)
    return by_psum(frontal, leading)


def solution(mesh):
    return jax.shard_map(
        functools.partial(body, mesh.shape["row"], mesh.shape["col"]),
        mesh=mesh,
        in_specs=(P(("front", "row"), None, "col"), P(("front", "row"))),
        out_specs=P("front", "col"),
        check_vma=False,
    )
```

time: 489 us -> 140 us (0.29)
  waiting for transfers between devices: 304 us -> 0 us
  Pallas kernels: 0 us -> 135 us
  other arithmetic: 130 us -> 1.37 us
  matrix products: 21.1 us -> 0 us
  between operations: 16.6 us -> 0.67 us
  local copies, waits for them, and re-layouts: 16.8 us -> 2.02 us
    psum x3 -> x0, waiting for transfers between devices: 304 us -> none  [the longest x1 168 us: body(): projected = lax.psum(inner_cols(first_basis, frontal), 'row')]
    pallas_call x0 -> x1, Pallas kernels: none -> 135 us  [by_kernel(): pl.pallas_call(functools.partial(kernel, n, leading), out_shape=jax.Shape...]
    another operation x17 -> x0, other arithmetic: 120 us -> none  [the longest x14 78.8 us: lower_factor(): return jnp.linalg.cholesky(gram)]
    another operation x17 -> x0, local copies, waits for them, and re-layouts: 14.2 us -> none
    another operation x13 -> x0, matrix products: 11.9 us -> none  [the longest x7 6.45 us: lower_inverse(): return jax.scipy.linalg.solve_triangular(factor, identity, lower=True)]
    dot_general x3 -> x0, matrix products: 9.2 us -> none  [the longest x2 8.02 us: inner_cols(): return jnp.einsum('rp,rc->pc', left, right, precision=lax.Precision.HIGHEST)]
    select_n x2 -> x0, other arithmetic: 5.85 us -> none  [the longest x1 5.13 us: body(): return jnp.where(kept_mask, projected, jnp.zeros_like(projected))]
  transfers between devices with their start and end apart: 3 -> 0, of which waited for: 3 -> 0; matrix products, arithmetic and copies ran while one was open for 0% -> 0% of each run, Pallas kernels for 0% -> 0%
where the time goes in v1:
time: 140 us; the launch traced here: 139 us
  Pallas kernels  135 us (96%)
  local copies, waits for them, and re-layouts  2.02 us (1%)
    pallas_call x1, Pallas kernels, by_kernel(): pl.pallas_call(functools.partial(kernel, n, leading), out_shape=jax.Shape...  135 us

profile of v1, /device:TPU:0, one launch (start us, length us, event | category | flops | bytes accessed | tf_op | source)
XLA Modules:
  0.0 139.4 jit_solution(11991786691087574139)
XLA Ops:
  0.7 1.4 select_bitcast_fusion.f_ref
  2.0 135.3 %front_rows.1 = f32[512,2048]{1,0:T(8,128)S(1)} custom-call(f32[128,2048]{1,0:T(8,128)S(1)} %select_bitcast_fusion.f_ref), custom_call_target="tpu_custom_call" | custom-call | tf_op jit(solution)/shard_map/front_rows/pallas_call | solution.py:267
  137.4 2.0 %copy.5 = f32[512,2048]{1,0:T(8,128)} copy(f32[512,2048]{1,0:T(8,128)S(1)} %front_rows.1) | data formatting | bytes 8388608
  (1 shorter events, 0.0 us)

commit v2 on v1

--- a/solution.py
+++ b/solution.py
@@ -46,31 +46,48 @@
 
 def inverse_factor(read, hooks):
     groups = LANES // SUB
-    row = lax.broadcasted_iota(jnp.int32, (SUB, LANES), 0)
-    col = lax.broadcasted_iota(jnp.int32, (SUB, LANES), 1)
+    tile = (SUB, LANES)
+    row = lax.broadcasted_iota(jnp.int32, tile, 0)
+    col = lax.broadcasted_iota(jnp.int32, tile, 1)
     a = [read(g) for g in range(groups)]
     b = [jnp.where(row + g * SUB == col, 1.0, 0.0).astype(jnp.float32) for g in range(groups)]
-    scales = []
-    for j in range(LANES):
-        if j in hooks:
-            hooks[j]()
-        home, i = divmod(j, SUB)
-        prow = a[home][i : i + 1, :]
-        brow = b[home][i : i + 1, :]
-        pinv = 1.0 / prow[:, j : j + 1]
-        srow = prow * pinv
-        trow = brow * pinv
-        for g in range(home, groups):
-            f = a[g][:, j : j + 1]
-            if g == home:
-                if i == SUB - 1:
-                    continue
-                f = jnp.where(row > i, jnp.broadcast_to(f, (SUB, LANES)), 0.0)
-            a[g] = a[g] - f * srow
-            b[g] = b[g] - f * trow
-        if i == SUB - 1:
-            diag = jnp.sum(jnp.where(row + home * SUB == col, a[home], 0.0), axis=1, keepdims=True)
-            b[home] = b[home] * lax.rsqrt(diag)
+
+    def columns(value, home):
+        first = home * SUB
+        return [jnp.broadcast_to(value[:, first + t : first + t + 1], tile) for t in range(SUB)]
+
+    def across(value, t):
+        return jnp.broadcast_to(value[t : t + 1, :], tile)
+
+    for home in range(groups):
+        if home in hooks:
+            hooks[home]()
+        f = columns(a[home], home)
+        arow, brow = a[home], b[home]
+        scaled, factors = [], []
+        diag = f[0]
+        for t in range(SUB):
+            pinv = 1.0 / across(f[t], t)
+            diag = jnp.where(row == t, f[t], diag)
+            srow = across(arow, t) * pinv
+            trow = across(brow, t) * pinv
+            later = [across(f[u], t) * pinv for u in range(t + 1, SUB)]
+            below = jnp.where(row > t, f[t], 0.0)
+            for u in range(t + 1, SUB):
+                f[u] = f[u] - below * later[u - t - 1]
+            if t < SUB - 1:
+                arow = arow - below * srow
+                brow = brow - below * trow
+            scaled.append((srow, trow))
+            factors.append(later)
+        b[home] = brow * lax.rsqrt(diag)
+        for g in range(home + 1, groups):
+            f = columns(a[g], home)
+            for t in range(SUB):
+                for u in range(t + 1, SUB):
+                    f[u] = f[u] - f[t] * factors[t][u - t - 1]
+                a[g] = a[g] - f[t] * scaled[t][0]
+                b[g] = b[g] - f[t] * scaled[t][1]
     return b
 
 
@@ -100,17 +117,18 @@
                 place = place + steps[s]
         return place
 
+    gc[...] = jnp.zeros_like(gc)
     barrier = pltpu.get_barrier_semaphore()
     for d in range(1, n):
         pl.semaphore_signal(barrier, inc=1, device_id={"row": lax.rem(r + d, n)}, device_id_type=MESH)
     pl.semaphore_signal(barrier, inc=1, device_id={"col": 1 - c}, device_id_type=MESH)
     pl.semaphore_wait(barrier, n)
 
-    mine = pl.ds(pl.multiple_of(r * height, height), height)
     lead = f_ref.at[:, pl.ds(0, leading)]
-    own_lead = pltpu.make_async_copy(lead, a_all.at[mine, :], own_sem.at[0])
+    first = pl.ds(0, height)
+    own_lead = pltpu.make_async_copy(lead, a_all.at[first, :], own_sem.at[0])
     to_pair = pltpu.make_async_remote_copy(
-        src_ref=lead, dst_ref=a_all.at[mine, :], send_sem=pair_send, recv_sem=pair_recv,
+        src_ref=lead, dst_ref=a_all.at[first, :], send_sem=pair_send, recv_sem=pair_recv,
         device_id={"col": 1 - c}, device_id_type=MESH,
     )
 
@@ -125,74 +143,89 @@
         to_pair.wait_recv()
 
     lead_steps = ordered(c)
-
-    def lead_half(j, core):
-        start = at(j, lead_steps) * height + core * half
-        return a_all.at[pl.ds(pl.multiple_of(start, half), half), :]
+    quarter = 1 << (stages - 2)
+
+    def lead_half(j):
+        low = j & (quarter - 1)
+        slot = low + ((j >> (stages - 2)) & 1) * quarter * (1 + c) + (j >> (stages - 1)) * quarter * (2 - c)
+        return a_all.at[pl.ds(pl.multiple_of(slot * height + c * half, half), half), :]
 
     def lead_copy(j, s):
+        k = j + (1 << s)
         return pltpu.make_async_remote_copy(
-            src_ref=lead_half(j, c), dst_ref=lead_half(j, c),
-            send_sem=ag_send.at[j + (1 << s)], recv_sem=ag_recv.at[j + (1 << s)],
+            src_ref=lead_half(j), dst_ref=lead_half(k), send_sem=ag_send.at[k], recv_sem=ag_recv.at[k],
             device_id={"row": r + lead_steps[s]}, device_id_type=MESH,
         )
 
     def core_copy(j):
         return pltpu.make_async_remote_copy(
-            src_ref=lead_half(j, c), dst_ref=lead_half(j, c),
+            src_ref=lead_half(j), dst_ref=lead_half(j),
             send_sem=core_send.at[j], recv_sem=core_recv.at[j],
             device_id={"col": 1 - c}, device_id_type=MESH,
         )
 
     def share_copy(d):
-        peer = lax.rem(r + d, n)
+        peer = at(d, deltas)
         return pltpu.make_async_remote_copy(
             src_ref=f_ref.at[:, pl.ds(pl.multiple_of(peer * share, share), share)],
-            dst_ref=f_all.at[mine, :],
+            dst_ref=f_all.at[pl.ds(d * height, height), :],
             send_sem=x_send.at[d], recv_sem=x_recv.at[d],
             device_id={"row": peer}, device_id_type=MESH,
         )
 
-    for s in range(stages):
-        lead_copy(0, s).start()
-    own_share = pltpu.make_async_copy(
-        f_ref.at[:, pl.ds(pl.multiple_of(r * share, share), share)], f_all.at[mine, :], own_sem.at[1]
-    )
-    own_share.start()
-    for d in range(1, n):
-        share_copy(d).start()
-    for j in range(1, n):
+    def take(j):
         top = j.bit_length() - 1
         lead_copy(j - (1 << top), top).wait_recv()
         for s in range(top + 1, stages):
             lead_copy(j, s).start()
         core_copy(j).start()
-    own_share.wait()
-    for j in range(1, n):
-        core_copy(j).wait_recv()
-    for d in range(1, n):
-        share_copy(d).wait_recv()
-
-    step_rows = 4 * LANES
-    gc[...] = jnp.zeros_like(gc)
-
-    @pl.loop(0, (n * height) // step_rows)
-    def _(t):
-        rows = pl.ds(pl.multiple_of(t * step_rows, step_rows), step_rows)
-        right = f_all[rows, :]
+
+    def gram(q):
+        rows = pl.ds(q * quarter * height, quarter * height)
         for k in range(chunks):
             ks = pl.ds(k * LANES, LANES)
-            left = a_all[rows, ks]
             rest = pl.ds(k * LANES, leading - k * LANES)
-            gc[ks, rest] += dot_t(left, a_all[rows, rest])
-            gc[ks, pl.ds(leading, share)] += dot_t(left, right)
+            gc[ks, rest] += dot_t(a_all[rows, ks], a_all[rows, rest])
+
+    for s in range(stages):
+        lead_copy(0, s).start()
+    own_share = pltpu.make_async_copy(
+        f_ref.at[:, pl.ds(pl.multiple_of(r * share, share), share)], f_all.at[first, :], own_sem.at[1]
+    )
+    own_share.start()
+    for j in range(1, 2 * quarter):
+        take(j)
+    for d in range(1, n):
+        share_copy(d).start()
+    for j in range(1, quarter):
+        core_copy(j).wait_recv()
+    gram(0)
+    for j in range(2 * quarter, 3 * quarter):
+        take(j)
+    for j in range(quarter, 3 * quarter):
+        core_copy(j).wait_recv()
+    gram(1)
+    for j in range(3 * quarter, n):
+        take(j)
+    gram(2)
+    for j in range(3 * quarter, n):
+        core_copy(j).wait_recv()
+    gram(3)
+
+    def products():
+        own_share.wait()
+        for d in range(1, n):
+            share_copy(d).wait_recv()
+        for q in range(n // quarter):
+            rows = pl.ds(q * quarter * height, quarter * height)
+            gc[:, pl.ds(leading, share)] += dot_t(a_all[rows, :], f_all[rows, :])
 
     def out_piece(k, j, steps):
         cols = pl.ds(pl.multiple_of(at(j, steps) * share, share), share)
         return out_ref.at[pl.ds(pl.multiple_of(k * LANES, LANES), LANES), cols]
 
     def out_copy(k, j, s):
-        steps = ordered(lax.rem(k, 2))
+        steps = ordered(lax.rem(k + c, 2))
         return pltpu.make_async_remote_copy(
             src_ref=out_piece(k, j, steps), dst_ref=out_piece(k, j, steps),
             send_sem=r_send.at[k, j + (1 << s)], recv_sem=r_recv.at[k, j + (1 << s)],
@@ -224,11 +257,12 @@
                     forward(k - 1, top)
             return run
 
-        gap = LANES // stages
-        hooks = {gap * (s + 1) - 1: hook(s) for s in range(stages)}
+        groups = LANES // SUB
+        hooks = {(groups * (s + 1)) // stages: hook(s) for s in range(stages - 1)}
         b = inverse_factor(read, hooks)
         for g, part in enumerate(b):
             inv[pl.ds(g * SUB, SUB), :] = part
+        pl.when(k == 0)(products)
         rows = jnp.dot(inv[...], gc[ks, :], precision=HIGHEST, preferred_element_type=jnp.float32)
         mine_out = rows[:, leading:]
         out_ref[ks, pl.ds(pl.multiple_of(r * share, share), share)] = jnp.where(
@@ -244,8 +278,10 @@
                 rest = pl.ds(i * LANES, leading + share - i * LANES)
                 gc[pl.ds(i * LANES, LANES), rest] -= dot_t(left, gc[ks, rest])
 
-    for top in range(stages):
+    for top in range(stages - 1):
         forward(chunks - 1, top)
+    for k in range(chunks):
+        forward(k, stages - 1)
 
     @pl.when(c == 0)
     def _():

time: 140 us -> 112 us (0.80)
  Pallas kernels: 135 us -> 108 us
    pallas_call x1, Pallas kernels: 135 us -> 108 us  [by_kernel(): pl.pallas_call(functools.partial(kernel, n, leading), out_shape=jax.Shape...]
where the time goes in v2:
time: 112 us
  Pallas kernels  108 us (96%)
  local copies, waits for them, and re-layouts  2.02 us (2%)
  other arithmetic  1.37 us (1%)
    pallas_call x1, Pallas kernels, by_kernel(): pl.pallas_call(functools.partial(kernel, n, leading), out_shape=jax.Shape...  108 us

profile of v2, /device:TPU:0, one launch (start us, length us, event | category | flops | bytes accessed | tf_op | source)
XLA Modules:
  0.0 112.1 jit_solution(10694132524088935000)
XLA Ops:
  0.7 1.4 %select_bitcast_fusion.f_ref = f32[128,2048]{1,0:T(8,128)S(1)} fusion(f32[1,128,2048]{2,1,0:T(8,128)} %param.2, pred[128]{0:T(512)(128)(4,1)S(1)} %iota_compare_fusion), kind=kLoop, calls=%fused_computation | loop fusion | flops 262144 | bytes 2097280 | tf_op jit(solution)/shard_map/reshape | solution.py:327
  2.0 108.1 %front_rows.1 = f32[512,2048]{1,0:T(8,128)S(1)} custom-call(f32[128,2048]{1,0:T(8,128)S(1)} %select_bitcast_fusion.f_ref), custom_call_target="tpu_custom_call" | custom-call | tf_op jit(solution)/shard_map/front_rows/pallas_call | solution.py:303
  110.1 2.0 %copy.5 = f32[512,2048]{1,0:T(8,128)} copy(f32[512,2048]{1,0:T(8,128)S(1)} %front_rows.1) | data formatting | bytes 8388608
  (1 shorter events, 0.0 us)

commit v3 on v2

--- a/solution.py
+++ b/solution.py
@@ -250,15 +250,17 @@
         def read(g):
             return gc[pl.ds(pl.multiple_of(base + g * SUB, SUB), SUB), ks]
 
-        def hook(top):
+        def hook(back, top):
             def run():
-                @pl.when(k > 0)
+                @pl.when(k >= back)
                 def _():
-                    forward(k - 1, top)
+                    forward(k - back, top)
             return run
 
         groups = LANES // SUB
-        hooks = {(groups * (s + 1)) // stages: hook(s) for s in range(stages - 1)}
+        hooks = {2: hook(2, stages - 2)}
+        for s in range(stages - 2):
+            hooks[groups * (s + 1) // (stages - 1) + 1] = hook(1, s)
         b = inverse_factor(read, hooks)
         for g, part in enumerate(b):
             inv[pl.ds(g * SUB, SUB), :] = part
@@ -278,6 +280,7 @@
                 rest = pl.ds(i * LANES, leading + share - i * LANES)
                 gc[pl.ds(i * LANES, LANES), rest] -= dot_t(left, gc[ks, rest])
 
+    forward(chunks - 2, stages - 2)
     for top in range(stages - 1):
         forward(chunks - 1, top)
     for k in range(chunks):

time: 112 us -> 102 us (0.911)
  Pallas kernels: 108 us -> 97.6 us
    pallas_call x1, Pallas kernels: 108 us -> 97.6 us  [by_kernel(): pl.pallas_call(functools.partial(kernel, n, leading), out_shape=jax.Shape...]
where the time goes in v3:
time: 102 us
  Pallas kernels  97.6 us (96%)
  local copies, waits for them, and re-layouts  2.02 us (2%)
  other arithmetic  1.37 us (1%)
    pallas_call x1, Pallas kernels, by_kernel(): pl.pallas_call(functools.partial(kernel, n, leading), out_shape=jax.Shape...  97.6 us

profile of v3, /device:TPU:0, one launch (start us, length us, event | category | flops | bytes accessed | tf_op | source)
XLA Modules:
  0.0 101.6 jit_solution(7630559179585392700)
XLA Ops:
  0.7 1.4 %select_bitcast_fusion.f_ref = f32[128,2048]{1,0:T(8,128)S(1)} fusion(f32[1,128,2048]{2,1,0:T(8,128)} %param.2, pred[128]{0:T(512)(128)(4,1)S(1)} %iota_compare_fusion), kind=kLoop, calls=%fused_computation | loop fusion | flops 262144 | bytes 2097280 | tf_op jit(solution)/shard_map/reshape | solution.py:330
  2.0 97.6 %front_rows.1 = f32[512,2048]{1,0:T(8,128)S(1)} custom-call(f32[128,2048]{1,0:T(8,128)S(1)} %select_bitcast_fusion.f_ref), custom_call_target="tpu_custom_call" | custom-call | tf_op jit(solution)/shard_map/front_rows/pallas_call | solution.py:306
  99.6 2.0 %copy.5 = f32[512,2048]{1,0:T(8,128)} copy(f32[512,2048]{1,0:T(8,128)S(1)} %front_rows.1) | data formatting | bytes 8388608
  (1 shorter events, 0.0 us)
